TPU v7x, 32 devices: a whole 2x2x4 slice. The times are simulated.
32 devices in a mesh: node: 4 (over y, x), local: 4 (over z), rep: 2 (over core).
Axes of the slice: x: 2, y: 2, z: 4, core: 2. Of those that a mesh axis runs over, the one named last changes fastest.
Arguments:
- grad_out: bfloat16 [256, 4096], P(('node', 'local', 'rep')), may hold values from -0.59765625 to 0.59765625
- expert_ids: int32 [256, 4], P(('node', 'local', 'rep')), may hold values from 0 to 15, as said below
- route_weights: bfloat16 [256, 4], P(('node', 'local', 'rep')), may hold values from 0.19921875 to 2
- gate_pre: bfloat16 [128, 16384], P('rep', ('node', 'local')), may hold values from -6 to 6
- up_pre: bfloat16 [128, 16384], P('rep', ('node', 'local')), may hold values from -6 to 6
- w_down_t: bfloat16 [4096, 16384], P(None, ('node', 'local')), may hold values from -0.1875 to 0.1875
Outputs:
- grad_gate_pre: bfloat16 [128, 16384], P('rep', ('node', 'local'))
- grad_up_pre: bfloat16 [128, 16384], P('rep', ('node', 'local'))
- grad_down_t: bfloat16 [4096, 16384], P('rep', ('node', 'local'))
- grad_route: bfloat16 [256, 16], P(('local', 'rep'), 'node')
Inputs may be any that keep to these rules, and one draw needn't show every extreme that they name: `expert_ids`: each token names 4 different experts: 2 in each of 2 different groups (group of e = e // 4). In every cohort each group is named by exactly 16 tokens, and within it exactly 1 expert are named 16 times, 2 experts 8 times and the others never. In every group one expert is named 16 times by every cohort.
All inputs are finite; a program needn't handle non-finite values.
Results may differ from a plain program's by a relative error of at most 0.013.
Values may be sent and summed in bfloat16 or wider, within the bound.
A program may use at most 64 MiB of HBM per device.

v0:
```python
import jax
import jax.numpy as jnp
from jax import lax
from jax.sharding import PartitionSpec as P

H = 1024


def swapped(block, axis, distance):
    count = lax.axis_size(axis)
    route = []
    for low in range(count):
        high = low | 1 << distance
        if high != low and high < count:
            route += [(low, high), (high, low)]
    return lax.ppermute(block, axis, route)


def outer_term(columns, weighted):
    return lax.dot_general(
        columns, weighted, (((0,), (0,)), ((), ())), preferred_element_type=jnp.float32
    )


def per_device(grad_out, expert_ids, route_weights, gate_pre, up_pre, w_down_t):
    tok_dev, width = grad_out.shape
    slot_rows, hidden_slice = gate_pre.shape
    node_count = lax.axis_size("node")
    local_count = lax.axis_size("local")
    owners = H // hidden_slice
    exp_group = local_count // owners
    experts = exp_group * node_count
    capacity = slot_rows // local_count
    expert_range = lax.iota(jnp.int32, experts)
    route_hits = expert_ids[:, :, None] == expert_range[None, None, :]
    dense_weights = jnp.sum(
        jnp.where(route_hits, route_weights[:, :, None].astype(jnp.float32), 0.0), axis=1
    ).astype(jnp.bfloat16)
    cohort_grad, cohort_weights = (
        lax.all_gather(grad_out, "node", axis=0, tiled=True),
        lax.all_gather(dense_weights, "node", axis=0, tiled=True),
    )
    group_index = lax.axis_index("node")
    group_weights = lax.dynamic_slice_in_dim(cohort_weights, group_index * exp_group, exp_group, 1)
    routed = (group_weights != 0).astype(jnp.int32)
    earlier = jnp.cumsum(routed, axis=0) - routed
    slot_range = lax.iota(jnp.int32, capacity)
    select = (routed[:, :, None] == 1) & (earlier[:, :, None] == slot_range[None, None, :])
    select_half = select.astype(jnp.bfloat16)
    packed = jnp.einsum(
        "cjs,cd->jsd", select_half, cohort_grad, preferred_element_type=jnp.float32
    ).astype(jnp.bfloat16)
    packed_weights = jnp.einsum(
        "cjs,cj->js", select_half, group_weights, preferred_element_type=jnp.float32
    ).astype(jnp.bfloat16)
    send_grad = jnp.broadcast_to(packed[:, None], (exp_group, owners, capacity, width)).reshape(
        local_count, capacity, width
    )
    send_weights = jnp.broadcast_to(packed_weights[:, None], (exp_group, owners, capacity)).reshape(
        local_count, capacity
    )
    recv_grad, recv_weights = (
        lax.all_to_all(send_grad, "local", split_axis=0, concat_axis=0, tiled=True),
        lax.all_to_all(send_weights, "local", split_axis=0, concat_axis=0, tiled=True),
    )
    cotangent = recv_grad.reshape(slot_rows, width)
    weight = recv_weights.reshape(slot_rows, 1).astype(jnp.float32)
    gate_value = gate_pre.astype(jnp.float32)
    up_value = up_pre.astype(jnp.float32)
    backward = jnp.dot(cotangent, w_down_t, preferred_element_type=jnp.float32)
    sigmoid_gate = jax.nn.sigmoid(gate_value)
    activated = gate_value * sigmoid_gate
    hidden = activated * up_value
    shares = jnp.sum(hidden * backward, axis=1).astype(jnp.bfloat16)
    scaled = weight * backward
    grad_gate_pre = (
        scaled * up_value * sigmoid_gate * (1.0 + gate_value * (1.0 - sigmoid_gate))
    ).astype(jnp.bfloat16)
    grad_up_pre = (scaled * activated).astype(jnp.bfloat16)
    weighted = (weight * hidden).astype(jnp.bfloat16)
    returned = lax.all_to_all(
        shares.reshape(local_count, capacity), "local", split_axis=0, concat_axis=0, tiled=True
    )
    slice_sum = jnp.sum(returned.astype(jnp.float32).reshape(exp_group, owners, capacity), axis=1)
    grad_route = jnp.sum(jnp.where(select, slice_sum[None], 0.0), axis=2).astype(jnp.bfloat16)
    half_width = width // lax.axis_size("rep")
    replica = lax.axis_index("rep")
    own_cols = lax.dynamic_slice_in_dim(cotangent, replica * half_width, half_width, 1)
    peer_cols = lax.dynamic_slice_in_dim(cotangent, (1 - replica) * half_width, half_width, 1)
    got_cols, got_weighted = swapped((peer_cols, weighted), "rep", 0)
    own_term = outer_term(own_cols, weighted).astype(jnp.bfloat16).astype(jnp.float32)
    peer_term = outer_term(got_cols, got_weighted).astype(jnp.bfloat16).astype(jnp.float32)
    grad_down_t = (own_term + peer_term).astype(jnp.bfloat16)
    return (grad_gate_pre, grad_up_pre, grad_down_t, grad_route)


def solution(mesh):
    placed = (
        P(("node", "local", "rep"), None),
        P(("node", "local", "rep"), None),
        P(("node", "local", "rep"), None),
        P("rep", ("node", "local")),
        P("rep", ("node", "local")),
        P(None, ("node", "local")),
    )
    return jax.shard_map(
        per_device,
        mesh=mesh,
        in_specs=placed,
        out_specs=(
            P("rep", ("node", "local")),
            P("rep", ("node", "local")),
            P("rep", ("node", "local")),
            P(("local", "rep"), "node"),
        ),
        check_vma=False,
    )
```

profile of v0, /device:TPU:0, one launch (start us, length us, event | category | flops | bytes accessed | tf_op | source)
XLA Modules:
  0.0 65.3 jit_solution(16456574721643578642)
XLA Ops:
  0.6 0.7 %convert_element_type.77 = f32[8,4]{0,1:T(4,128)S(1)} convert(bf16[8,4]{0,1:T(4,128)(2,1)} %param.8) | non-fusion elementwise | flops 32 | bytes 192 | tf_op jit(solution)/shard_map/convert_element_type | solution.py:37
  1.3 0.8 %select_reduce_fusion.1 = bf16[8,16]{1,0:T(8,128)(2,1)S(1)} fusion(f32[8,4]{0,1:T(4,128)S(1)} %convert_element_type.77, s32[8,4]{0,1:T(4,128)} %param.7), kind=kLoop, calls=%fused_computation.26 | loop fusion | flops 1408 | bytes 512 | tf_op jit(solution)/shard_map/reduce_sum | solution.py:36
  2.1 9.6 %all_gather.6 = bf16[32,16]{1,0:T(8,128)(2,1)S(1)} all-gather(bf16[8,16]{1,0:T(8,128)(2,1)S(1)} %select_reduce_fusion.1), channel_id=1, replica_groups=mesh['node'=4,'local'=4,'rep'=2] {'node'}, dimensions={0}, use_global_device_ids=true | all-gather | bytes 1280 | tf_op jit(solution)/shard_map/all_gather | solution.py:41
  11.7 0.1 broadcast_compare_fusion
  11.7 0.1 dynamic-slice_bitcast_fusion
  11.8 0.1 reduce_window_sum.11
  11.9 0.1 fusion.18
  11.9 0.1 copy.21
  12.0 0.1 copy.20
  12.1 0.1 copy.24
  12.2 0.1 fusion.12
  12.4 0.6 copy.22
  13.0 4.9 %all-to-all-start = ((bf16[4,1,16]{2,1,0:T(2,128)(2,1)}), bf16[4,1,16]{2,1,0:T(2,128)(2,1)S(1)}, u32[]{:S(2)}, u32[]{:S(2)}) async-start(bf16[4,1,16]{2,1,0:T(2,128)(2,1)} %copy.22), calls=%async_computation | async-start | bytes 4096 | tf_op jit(solution)/shard_map/all_to_all | solution.py:64
  17.8 9.0 %all_gather.7 = bf16[32,4096]{1,0:T(8,128)(2,1)S(1)} all-gather(bf16[8,4096]{1,0:T(8,128)(2,1)} %param.6), channel_id=1, replica_groups=mesh['node'=4,'local'=4,'rep'=2] {'node'}, dimensions={0}, use_global_device_ids=true | all-gather | bytes 327680 | tf_op jit(solution)/shard_map/all_gather | solution.py:40
  26.8 1.1 %convolution_convert_fusion = bf16[4,16,4096]{2,1,0:T(8,128)(2,1)} fusion(bf16[32,4096]{1,0:T(8,128)(2,1)S(1)} %all_gather.7, s32[32,4]{0,1:T(4,128)S(1)} %copy.21, pred[32,4]{0,1:T(4,128)(4,1)S(1)} %copy.20), kind=kOutput, calls=%fused_computation.1 | convolution fusion | flops 17043456 | bytes 787072 | tf_op jit(solution)/shard_map/cjs,cd->jsd/dot_general | solution.py:50
  27.9 0.0 all-to-all-done
  27.9 5.1 %all-to-all-start.1 = ((bf16[4,16,4096]{2,1,0:T(8,128)(2,1)}), bf16[4,16,4096]{2,1,0:T(8,128)(2,1)S(1)}, u32[]{:S(2)}, u32[]{:S(2)}) async-start(bf16[4,16,4096]{2,1,0:T(8,128)(2,1)} %convolution_convert_fusion), calls=%async_computation.1 | async-start | bytes 1048576 | tf_op jit(solution)/shard_map/all_to_all | solution.py:63
  33.0 0.1 reshape.50
  33.1 10.2 %all-to-all-done.1 = bf16[4,16,4096]{2,1,0:T(8,128)(2,1)S(1)} async-done(((bf16[4,16,4096]{2,1,0:T(8,128)(2,1)}), bf16[4,16,4096]{2,1,0:T(8,128)(2,1)S(1)}, u32[]{:S(2)}, u32[]{:S(2)}) %all-to-all-start.1) | async-done | bytes 524320 | tf_op jit(solution)/shard_map/all_to_all | solution.py:63
  43.2 6.0 %multiply_reduce_fusion = (bf16[64]{0:T(256)(128)(2,1)S(1)}, bf16[64,1024]{1,0:T(8,128)(2,1)}, bf16[64,1024]{1,0:T(8,128)(2,1)}, bf16[64,1024]{1,0:T(8,128)(2,1)S(1)}) fusion(bf16[64,1024]{1,0:T(8,128)(2,1)} %param.10, bf16[64,1024]{1,0:T(8,128)(2,1)} %param.9, f32[64]{0:T(128)S(1)} %reshape.50, bf16[64,4096]{1,0:T(8,128)(2,1)S(1)} %bitcast.17, ...), kind=kOutput, calls=%fused_computation.15 | convolution fusion | flops 538247104 | bytes 9568640 | tf_op jit(solution)/shard_map/dot_general | solution.py:70
  49.2 0.1 collective-permute-start.1
  49.3 0.5 collective-permute-start
  49.9 0.7 %convert_element_type.98 = bf16[4,1,16]{2,1,0:T(2,128)(2,1)} reshape(bf16[64]{0:T(256)(128)(2,1)S(1)} %get-tuple-element.4) | data formatting | bytes 256 | tf_op jit(solution)/shard_map/convert_element_type | solution.py:74
  50.5 3.2 %all-to-all-start.2 = ((bf16[4,1,16]{2,1,0:T(2,128)(2,1)}), bf16[4,1,16]{2,1,0:T(2,128)(2,1)S(1)}, u32[]{:S(2)}, u32[]{:S(2)}) async-start(bf16[4,1,16]{2,1,0:T(2,128)(2,1)} %convert_element_type.98), calls=%async_computation.2 | async-start | bytes 4096 | tf_op jit(solution)/shard_map/all_to_all | solution.py:81
  53.8 3.3 %fusion.8 = bf16[2048,1024]{1,0:T(8,128)(2,1)} fusion(bf16[64,1024]{1,0:T(8,128)(2,1)S(1)} %get-tuple-element.7, bf16[64,4096]{1,0:T(8,128)(2,1)S(1)} %bitcast.19, s32[]{:T(128)S(6)} %select_n.19), kind=kOutput, calls=%fused_computation.17 | convolution fusion | flops 268435456 | bytes 4587524 | tf_op jit(solution)/shard_map/dot_general | solution.py:20
  57.1 2.1 %all-to-all-done.2 = bf16[4,1,16]{2,1,0:T(2,128)(2,1)S(1)} async-done(((bf16[4,1,16]{2,1,0:T(2,128)(2,1)}), bf16[4,1,16]{2,1,0:T(2,128)(2,1)S(1)}, u32[]{:S(2)}, u32[]{:S(2)}) %all-to-all-start.2) | async-done | bytes 160 | tf_op jit(solution)/shard_map/all_to_all | solution.py:81
  59.2 0.7 %select_reduce_fusion = bf16[32,4]{0,1:T(4,128)(2,1)} fusion(f32[4,16]{1,0:T(4,128)S(1)} %bitcast.20, s32[32,4]{0,1:T(4,128)S(1)} %copy.21, pred[32,4]{0,1:T(4,128)(4,1)S(1)} %copy.20), kind=kLoop, calls=%fused_computation.20 | loop fusion | flops 8064 | bytes 1152 | tf_op jit(solution)/shard_map/reduce_sum | solution.py:85
  59.8 0.0 collective-permute-done.1
  59.8 0.0 collective-permute-done
  59.9 5.5 %add_convert_fusion = bf16[2048,1024]{1,0:T(8,128)(2,1)} fusion(bf16[2048,1024]{1,0:T(8,128)(2,1)} %fusion.8, bf16[64,2048]{1,0:T(8,128)(2,1)S(1)} %collective-permute-done, bf16[64,1024]{1,0:T(8,128)(2,1)S(1)} %collective-permute-done.1), kind=kOutput, calls=%fused_computation | convolution fusion | flops 278921216 | bytes 8781824 | tf_op jit(solution)/shard_map/dot_general | solution.py:20
  (4 shorter events, 0.1 us)
Async XLA Ops:
  13.0 14.9 %all-to-all-start = ((bf16[4,1,16]{2,1,0:T(2,128)(2,1)}), bf16[4,1,16]{2,1,0:T(2,128)(2,1)S(1)}, u32[]{:S(2)}, u32[]{:S(2)}) async-start(bf16[4,1,16]{2,1,0:T(2,128)(2,1)} %copy.22), calls=%async_computation | async-start | bytes 4096 | tf_op jit(solution)/shard_map/all_to_all | solution.py:64
  27.9 15.4 %all-to-all-start.1 = ((bf16[4,16,4096]{2,1,0:T(8,128)(2,1)}), bf16[4,16,4096]{2,1,0:T(8,128)(2,1)S(1)}, u32[]{:S(2)}, u32[]{:S(2)}) async-start(bf16[4,16,4096]{2,1,0:T(8,128)(2,1)} %convolution_convert_fusion), calls=%async_computation.1 | async-start | bytes 1048576 | tf_op jit(solution)/shard_map/all_to_all | solution.py:63
  49.2 10.6 %collective-permute-start.1 = (bf16[64,1024]{1,0:T(8,128)(2,1)S(1)}, bf16[64,1024]{1,0:T(8,128)(2,1)S(1)}, u32[]{:S(2)}, u32[]{:S(2)}) collective-permute-start(bf16[64,1024]{1,0:T(8,128)(2,1)S(1)} %get-tuple-element.7), channel_id=1, source_target_pairs={{0,1},{1,0},{2,3},{3,2},{4,5},{5,4},{6,7},{7,6},{8,9},{9,8},{10,11... | collective-permute-start | bytes 393224 | tf_op jit(solution)/shard_map/ppermute | solution.py:16
  49.3 10.5 %collective-permute-start = (bf16[64,2048]{1,0:T(8,128)(2,1)S(1)}, bf16[64,2048]{1,0:T(8,128)(2,1)S(1)}, u32[]{:S(2)}, u32[]{:S(2)}) collective-permute-start(bf16[64,2048]{1,0:T(8,128)(2,1)S(1)} %constant_dynamic-slice_fusion), channel_id=1, source_target_pairs={{0,1},{1,0},{2,3},{3,2},{4,5},{5,4},{6,7},{7,6},{8,9},{9,8},{10,11... | collective-permute-start | bytes 786440 | tf_op jit(solution)/shard_map/ppermute | solution.py:16
  50.5 8.6 %all-to-all-start.2 = ((bf16[4,1,16]{2,1,0:T(2,128)(2,1)}), bf16[4,1,16]{2,1,0:T(2,128)(2,1)S(1)}, u32[]{:S(2)}, u32[]{:S(2)}) async-start(bf16[4,1,16]{2,1,0:T(2,128)(2,1)} %convert_element_type.98), calls=%async_computation.2 | async-start | bytes 4096 | tf_op jit(solution)/shard_map/all_to_all | solution.py:81
where the time goes:
time: 65.8 us; the launch traced here: 65.3 us
  blocking collectives  18.5 us (28%)
  matrix products  16 us (24%)
  starting transfers between devices  13.8 us (21%)
  waiting for transfers between devices  12.3 us (19%)
  other arithmetic  2.34 us (4%)
  local copies, waits for them, and re-layouts  1.72 us (3%)
  between operations  0.68 us (1%)
    all_to_all x1, waiting for transfers between devices, per_device(): lax.all_to_all(send_grad, 'local', split_axis=0, concat_axis=0, tiled=True)  10.2 us
    all_gather x1, blocking collectives, per_device(): lax.all_gather(dense_weights, 'node', axis=0, tiled=True)  9.57 us
    all_gather x1, blocking collectives, per_device(): lax.all_gather(grad_out, 'node', axis=0, tiled=True)  8.95 us
    dot_general x2, matrix products, outer_term(): lax.dot_general(columns, weighted, (((0,), (0,)), ((), ())), preferred_el...  8.78 us
    dot_general x1, matrix products, per_device(): backward = jnp.dot(cotangent, w_down_t, preferred_element_type=jnp.float32)  5.96 us
    all_to_all x1, starting transfers between devices, per_device(): lax.all_to_all(send_grad, 'local', split_axis=0, concat_axis=0, tiled=True)  5.1 us
    all_to_all x1, starting transfers between devices, per_device(): lax.all_to_all(send_weights, 'local', split_axis=0, concat_axis=0, tiled=...  4.87 us
    all_to_all x1, starting transfers between devices, per_device(): lax.all_to_all(shares.reshape(local_count, capacity), 'local', split_axis...  3.24 us
  transfers between devices with their start and end apart: 5, of which 2 were waited for; matrix products, arithmetic and copies ran while one was open for 9% of the time, Pallas kernels for 0%

commit v1 on v0

--- a/solution.py
+++ b/solution.py
@@ -1,9 +1,348 @@
+import functools
 import jax
 import jax.numpy as jnp
 from jax import lax
+from jax.experimental import pallas as pl
+from jax.experimental.pallas import tpu as pltpu
 from jax.sharding import PartitionSpec as P
 
 H = 1024
+PER_GROUP = 2
+CHUNKS = 4
+MESH = pl.DeviceIdType.MESH
+F32 = jnp.float32
+BF16 = jnp.bfloat16
+KERNEL_PARAMS = dict(vmem_limit_bytes=40 * 1024 * 1024)
+
+
+def contract_rows(left, right):
+    return lax.dot_general(left, right, (((0,), (0,)), ((), ())), preferred_element_type=F32)
+
+
+def one_hot(member, column, width):
+    lanes = lax.broadcasted_iota(jnp.int32, (member.shape[0], width), 1).astype(F32)
+    return jnp.where((member > 0) & (column == lanes), 1.0, 0.0).astype(BF16)
+
+
+def lower_triangle(rows, block):
+    row = lax.broadcasted_iota(jnp.int32, (rows, rows), 0)
+    col = lax.broadcasted_iota(jnp.int32, (rows, rows), 1)
+    return jnp.where((col < row) & (row // block == col // block), 1.0, 0.0).astype(BF16)
+
+
+def routed_kernel(
+    dims, ids_ref, rw_ref, grad_ref, gate_ref, up_ref, w_ref,
+    cot_out, wtd_out, ggate_out, gup_out, route_out,
+    ids_buf, rw_buf, coh, gath, peer_cot, w_buf, gate_buf, up_buf, acc, share_buf, back_buf,
+    load_sem, w_sem, own_sem,
+    ids_send, ids_recv, rw_send, rw_recv, coh_send, coh_recv,
+    zids_send, zids_recv, zrw_send, zrw_recv,
+    right_send, right_recv, left_send, left_recv,
+    wtd_send, wtd_recv, cot_send, cot_recv, share_send, share_recv,
+):
+    nodes, locals_, tok, top, width, hs, group_tok, owners = dims
+    cohort = nodes * tok
+    exp_group = locals_ // owners
+    slots = gate_ref.shape[0]
+    capacity = slots // locals_
+    half = width // 2
+    cw = width // CHUNKS
+    half_chunks = CHUNKS // 2
+    me_n, me_l, me_r = lax.axis_index("node"), lax.axis_index("local"), lax.axis_index("rep")
+    peer = {"rep": 1 - me_r}
+
+    def node_at(k):
+        return {"node": lax.rem(me_n + k, nodes)}
+
+    def local_at(k):
+        return {"local": lax.rem(me_l + k, locals_)}
+
+    def remote(src, dst, send, recv, device):
+        return pltpu.make_async_remote_copy(
+            src_ref=src, dst_ref=dst, send_sem=send, recv_sem=recv,
+            device_id=device, device_id_type=MESH,
+        )
+
+    barrier = pltpu.get_barrier_semaphore()
+    for k in range(1, nodes):
+        pl.semaphore_signal(barrier, inc=1, device_id=node_at(k), device_id_type=MESH)
+    for k in range(1, locals_):
+        pl.semaphore_signal(barrier, inc=1, device_id=local_at(k), device_id_type=MESH)
+    pl.semaphore_signal(barrier, inc=1, device_id=peer, device_id_type=MESH)
+
+    def cols(c):
+        return pl.ds(c * cw, cw)
+
+    own_copies = [
+        pltpu.make_async_copy(ids_ref, ids_buf.at[me_l, me_n], own_sem.at[0]),
+        pltpu.make_async_copy(rw_ref, rw_buf.at[me_l, me_n], own_sem.at[1]),
+        pltpu.make_async_copy(grad_ref, coh.at[me_n], own_sem.at[2]),
+    ]
+    for copy in own_copies:
+        copy.start()
+    gate_copy = pltpu.make_async_copy(gate_ref, gate_buf, load_sem.at[0])
+    up_copy = pltpu.make_async_copy(up_ref, up_buf, load_sem.at[1])
+    gate_copy.start()
+    up_copy.start()
+    w_copies = [
+        pltpu.make_async_copy(w_ref.at[cols(c), :], w_buf.at[cols(c), :], w_sem.at[c])
+        for c in range(CHUNKS)
+    ]
+    pl.semaphore_wait(barrier, nodes + locals_ - 1)
+
+    ids_copies, rw_copies, coh_copies = [], [], {}
+    for k in range(1, nodes):
+        ids_copies.append(remote(ids_ref, ids_buf.at[me_l, me_n], ids_send.at[k], ids_recv.at[k], node_at(k)))
+        rw_copies.append(remote(rw_ref, rw_buf.at[me_l, me_n], rw_send.at[k], rw_recv.at[k], node_at(k)))
+    for copy in ids_copies + rw_copies:
+        copy.start()
+    for c in range(CHUNKS):
+        for k in range(1, nodes):
+            copy = remote(
+                grad_ref.at[:, cols(c)], coh.at[me_n, :, cols(c)],
+                coh_send.at[c, k], coh_recv.at[c, k], node_at(k),
+            )
+            copy.start()
+            coh_copies[c, k] = copy
+    for copy in w_copies:
+        copy.start()
+    for copy in own_copies:
+        copy.wait()
+    for copy in ids_copies + rw_copies:
+        copy.wait_recv()
+    zids_copies, zrw_copies = [], []
+    for k in range(1, locals_):
+        zids_copies.append(remote(ids_buf.at[me_l], ids_buf.at[me_l], zids_send.at[k], zids_recv.at[k], local_at(k)))
+        zrw_copies.append(remote(rw_buf.at[me_l], rw_buf.at[me_l], zrw_send.at[k], zrw_recv.at[k], local_at(k)))
+    for copy in zids_copies + zrw_copies:
+        copy.start()
+
+    own_ids = ids_buf[me_l].reshape(cohort, top)
+    lanes = lax.broadcasted_iota(jnp.int32, (cohort, 128), 1)
+    first = me_n * exp_group
+    hits = jnp.zeros((cohort, 128), F32)
+    for k in range(top):
+        hits = hits + jnp.where((own_ids[:, k:k + 1] - first == lanes) & (lanes < exp_group), 1.0, 0.0)
+    in_group = jnp.where(jnp.sum(hits, axis=1, keepdims=True) > 0, 1.0, 0.0)
+    hits = jnp.where(lanes == exp_group, in_group, hits)
+    before = jnp.dot(lower_triangle(cohort, cohort), hits.astype(BF16), preferred_element_type=F32)
+    pick = one_hot(in_group, before[:, exp_group:exp_group + 1], group_tok)
+
+    def shifted(buf, copies_send, copies_recv, source, d, c, step):
+        return remote(
+            buf.at[source, :, cols(c)], buf.at[source, :, cols(c)],
+            copies_send.at[d - 1, c], copies_recv.at[d - 1, c], {"local": me_l + step},
+        )
+
+    def right(source, d, c):
+        return shifted(gath, right_send, right_recv, source, d, c, 1)
+
+    def left(source, d, c):
+        return shifted(gath, left_send, left_recv, source, d, c, -1)
+
+    state = {}
+
+    def prepare():
+        for copy in zids_copies + zrw_copies:
+            copy.wait_recv()
+        total = locals_ * cohort
+        all_ids = ids_buf[...].reshape(total, top)
+        all_rw = rw_buf[...].astype(F32).reshape(total, top)
+        expert = first + me_l // owners
+        match = jnp.where(all_ids == expert, 1.0, 0.0)
+        member = jnp.sum(match, axis=1, keepdims=True)
+        row_weight = jnp.sum(match * all_rw, axis=1, keepdims=True)
+        near = jnp.where((all_ids >= first) & (all_ids < first + exp_group), 1.0, 0.0)
+        grouped = jnp.where(jnp.sum(near, axis=1, keepdims=True) > 0, 1.0, 0.0)
+        lane = lax.broadcasted_iota(jnp.int32, (total, 128), 1)
+        both = jnp.where(lane == 0, member, jnp.where(lane == 1, grouped, 0.0)).astype(BF16)
+        earlier = jnp.dot(lower_triangle(total, cohort), both, preferred_element_type=F32)
+        which = (lax.broadcasted_iota(jnp.int32, (total, 1), 0) // cohort).astype(F32)
+        slot_hot = one_hot(member, earlier[:, 0:1] + which * capacity, slots)
+        pack_hot = one_hot(grouped, earlier[:, 1:2] + which * group_tok, locals_ * group_tok)
+        state["select"] = contract_rows(slot_hot, pack_hot).astype(BF16)
+        weight = contract_rows(slot_hot, jnp.broadcast_to(row_weight, (total, 128)).astype(BF16))[:, 0:1]
+        state["weight"] = weight
+        gate_copy.wait()
+        up_copy.wait()
+        gate = gate_buf[...].astype(F32)
+        hidden = gate * jax.nn.sigmoid(gate) * up_buf[...].astype(F32)
+        wtd_out[0:slots, :] = (weight * hidden).astype(BF16)
+
+    wtd_copy = remote(wtd_out.at[0:slots, :], wtd_out.at[slots:2 * slots, :], wtd_send, wtd_recv, peer)
+
+    def cot_copy(c):
+        part = pl.ds((c % half_chunks) * cw, cw)
+        return remote(
+            peer_cot.at[:, part], cot_out.at[slots:2 * slots, part],
+            cot_send.at[c % half_chunks], cot_recv.at[c % half_chunks], peer,
+        )
+
+    def finish(c):
+        rows = gath[:, :, cols(c)].reshape(locals_ * group_tok, cw)
+        cot = jnp.dot(state["select"], rows, preferred_element_type=F32).astype(BF16)
+        part = pl.ds((c % half_chunks) * cw, cw)
+
+        @pl.when(me_r == c // half_chunks)
+        def _():
+            cot_out[0:slots, part] = cot
+
+        @pl.when(me_r != c // half_chunks)
+        def _():
+            peer_cot[:, part] = cot
+
+        w_copies[c].wait()
+        term = jnp.dot(cot, w_buf[cols(c), :], preferred_element_type=F32)
+        if c == 0:
+            acc[...] = term
+        else:
+            acc[...] += term
+
+        @pl.when(me_r != c // half_chunks)
+        def _():
+            cot_copy(c).start()
+
+    for step in range(CHUNKS + locals_ - 1):
+        if step < CHUNKS:
+            for k in range(1, nodes):
+                coh_copies[step, k].wait_recv()
+            rows = coh[:, :, cols(step)].astype(F32).reshape(cohort, cw).astype(BF16)
+            gath[me_l, :, cols(step)] = contract_rows(pick, rows).astype(BF16)
+
+            @pl.when(me_l + 1 < locals_)
+            def _():
+                right(me_l, 1, step).start()
+
+            @pl.when(me_l > 0)
+            def _():
+                left(me_l, 1, step).start()
+
+        for d in range(1, locals_):
+            c = step - d
+            if not 0 <= c < CHUNKS:
+                continue
+
+            @pl.when(me_l >= d)
+            def _():
+                right(me_l - d, d, c).wait_recv()
+                if d < locals_ - 1:
+                    @pl.when(me_l + 1 < locals_)
+                    def _():
+                        right(me_l - d, d + 1, c).start()
+
+            @pl.when(me_l + d < locals_)
+            def _():
+                left(me_l + d, d, c).wait_recv()
+                if d < locals_ - 1:
+                    @pl.when(me_l > 0)
+                    def _():
+                        left(me_l + d, d + 1, c).start()
+
+        if step == locals_ - 2:
+            prepare()
+        if step >= locals_ - 1:
+            finish(step - locals_ + 1)
+            if step == locals_ - 1:
+                wtd_copy.start()
+
+    weight = state["weight"]
+    gate = gate_buf[...].astype(F32)
+    up = up_buf[...].astype(F32)
+    back = acc[...]
+    sig = jax.nn.sigmoid(gate)
+    act = gate * sig
+    shares = jnp.sum(act * up * back, axis=1, keepdims=True)
+    share_buf[...] = jnp.broadcast_to(shares, (slots, 128)).astype(BF16).reshape(locals_, capacity, 128)
+    scaled = weight * back
+    ggate_out[...] = (scaled * up * sig * (1.0 + gate * (1.0 - sig))).astype(BF16)
+    gup_out[...] = (scaled * act).astype(BF16)
+    back_buf[me_l] = share_buf[me_l]
+    share_copies = [
+        remote(share_buf.at[lax.rem(me_l + k, locals_)], back_buf.at[me_l], share_send.at[k], share_recv.at[k], local_at(k))
+        for k in range(1, locals_)
+    ]
+    for copy in share_copies:
+        copy.start()
+
+    for copy in ids_copies + rw_copies + zids_copies + zrw_copies + list(coh_copies.values()):
+        copy.wait_send()
+    for c in range(CHUNKS):
+        @pl.when(me_l + 1 < locals_)
+        def _():
+            for d in range(locals_ - 1):
+                @pl.when(me_l >= d)
+                def _():
+                    right(me_l - d, d + 1, c).wait_send()
+
+        @pl.when(me_l > 0)
+        def _():
+            for d in range(locals_ - 1):
+                @pl.when(me_l + d < locals_)
+                def _():
+                    left(me_l + d, d + 1, c).wait_send()
+    wtd_copy.wait()
+    for c in range(half_chunks):
+        cot_copy(c).wait()
+    for copy in share_copies:
+        copy.wait()
+    route = jnp.zeros((cohort, 128), F32)
+    for j in range(exp_group):
+        chosen = one_hot(hits[:, j:j + 1], before[:, j:j + 1], capacity)
+        value = jnp.zeros((cohort, 128), F32)
+        for o in range(owners):
+            value = value + jnp.dot(chosen, back_buf[j * owners + o], preferred_element_type=F32)
+        route = jnp.where(lanes == j, value, route)
+    route_out[...] = route[:, 0:exp_group].astype(BF16)
+
+
+def gathered(nodes, locals_, group_tok, grad_out, expert_ids, route_weights, gate_pre, up_pre, w_down_t):
+    tok, width = grad_out.shape
+    top = expert_ids.shape[1]
+    slots, hs = gate_pre.shape
+    owners = H // hs
+    exp_group = locals_ // owners
+    cohort = nodes * tok
+    capacity = slots // locals_
+    half = width // 2
+    dims = (nodes, locals_, tok, top, width, hs, group_tok, owners)
+    dma = pltpu.SemaphoreType.DMA
+    cot, weighted, grad_gate, grad_up, grad_route = pl.pallas_call(
+        functools.partial(routed_kernel, dims),
+        out_shape=(
+            jax.ShapeDtypeStruct((2 * slots, half), BF16),
+            jax.ShapeDtypeStruct((2 * slots, hs), BF16),
+            jax.ShapeDtypeStruct((slots, hs), BF16),
+            jax.ShapeDtypeStruct((slots, hs), BF16),
+            jax.ShapeDtypeStruct((cohort, exp_group), BF16),
+        ),
+        in_specs=[pl.BlockSpec(memory_space=pl.ANY)] * 6,
+        out_specs=tuple([pl.BlockSpec(memory_space=pltpu.VMEM)] * 5),
+        scratch_shapes=[
+            pltpu.VMEM((locals_, nodes, tok, top), jnp.int32),
+            pltpu.VMEM((locals_, nodes, tok, top), BF16),
+            pltpu.VMEM((nodes, tok, width), BF16),
+            pltpu.VMEM((locals_, group_tok, width), BF16),
+            pltpu.VMEM((slots, half), BF16),
+            pltpu.VMEM((width, hs), BF16),
+            pltpu.VMEM((slots, hs), BF16),
+            pltpu.VMEM((slots, hs), BF16),
+            pltpu.VMEM((slots, hs), F32),
+            pltpu.VMEM((locals_, capacity, 128), BF16),
+            pltpu.VMEM((locals_, capacity, 128), BF16),
+            dma((2,)), dma((CHUNKS,)), dma((3,)),
+            dma((nodes,)), dma((nodes,)), dma((nodes,)), dma((nodes,)),
+            dma((CHUNKS, nodes)), dma((CHUNKS, nodes)),
+            dma((locals_,)), dma((locals_,)), dma((locals_,)), dma((locals_,)),
+            dma((locals_ - 1, CHUNKS)), dma((locals_ - 1, CHUNKS)),
+            dma((locals_ - 1, CHUNKS)), dma((locals_ - 1, CHUNKS)),
+            dma(()), dma(()), dma((CHUNKS // 2,)), dma((CHUNKS // 2,)),
+            dma((locals_,)), dma((locals_,)),
+        ],
+        compiler_params=pltpu.CompilerParams(collective_id=0, has_side_effects=True, **KERNEL_PARAMS),
+        name="routed",
+    )(expert_ids, route_weights, grad_out, gate_pre, up_pre, w_down_t)
+    grad_down = contract_rows(cot, weighted).astype(BF16)
+    return grad_gate, grad_up, grad_down, grad_route
 
 
 def swapped(block, axis, distance):
@@ -22,7 +361,7 @@
     )
 
 
-def per_device(grad_out, expert_ids, route_weights, gate_pre, up_pre, w_down_t):
+def exchanged(grad_out, expert_ids, route_weights, gate_pre, up_pre, w_down_t):
     tok_dev, width = grad_out.shape
     slot_rows, hidden_slice = gate_pre.shape
     node_count = lax.axis_size("node")
@@ -94,6 +433,16 @@
     return (grad_gate_pre, grad_up_pre, grad_down_t, grad_route)
 
 
+def per_device(grad_out, expert_ids, route_weights, gate_pre, up_pre, w_down_t):
+    nodes, locals_ = lax.axis_size("node"), lax.axis_size("local")
+    capacity = gate_pre.shape[0] // locals_
+    group_tok = grad_out.shape[0] * expert_ids.shape[1] // PER_GROUP
+    args = (grad_out, expert_ids, route_weights, gate_pre, up_pre, w_down_t)
+    if group_tok > capacity:
+        return exchanged(*args)
+    return gathered(nodes, locals_, group_tok, *args)
+
+
 def solution(mesh):
     placed = (
         P(("node", "local", "rep"), None),

time: 65.8 us -> 45.6 us (0.69)
  Pallas kernels: 0 us -> 31.8 us
  blocking collectives: 18.5 us -> 0 us
  starting transfers between devices: 13.8 us -> 0 us
  matrix products: 16 us -> 3.29 us
  waiting for transfers between devices: 12.3 us -> 0 us
  local copies, waits for them, and re-layouts: 1.72 us -> 9.51 us
  other arithmetic: 2.34 us -> 0 us
    pallas_call x0 -> x1, Pallas kernels: none -> 31.8 us  [gathered(): pl.pallas_call(functools.partial(routed_kernel, dims), out_shape=(jax.Sha...]
    all_gather x2 -> x0, blocking collectives: 18.5 us -> none  [the longest x1 9.57 us: per_device(): lax.all_gather(dense_weights, 'node', axis=0, tiled=True)]
    all_to_all x3 -> x0, starting transfers between devices: 13.2 us -> none  [the longest x1 5.1 us: per_device(): lax.all_to_all(send_grad, 'local', split_axis=0, concat_axis=0, tiled=True)]
    dot_general x5 -> x1, matrix products: 16 us -> 3.29 us  [contract_rows(): lax.dot_general(left, right, (((0,), (0,)), ((), ())), preferred_element_...]
    all_to_all x3 -> x0, waiting for transfers between devices: 12.3 us -> none  [the longest x1 10.2 us: per_device(): lax.all_to_all(send_grad, 'local', split_axis=0, concat_axis=0, tiled=True)]
    unnamed x0 -> x13, local copies, waits for them, and re-layouts: none -> 9.51 us
    reduce_sum x2 -> x0, other arithmetic: 1.41 us -> none  [the longest x1 0.76 us: per_device(): jnp.sum(jnp.where(route_hits, route_weights[:, :, None].astype(jnp.float3...]
    convert_element_type x2 -> x0, local copies, waits for them, and re-layouts: 0.76 us -> none  [the longest x1 0.68 us: per_device(): shares = jnp.sum(hidden * backward, axis=1).astype(jnp.bfloat16)]
  transfers between devices with their start and end apart: 5 -> 0, of which waited for: 2 -> 0; matrix products, arithmetic and copies ran while one was open for 9% -> 0% of each run, Pallas kernels for 0% -> 0%
where the time goes in v1:
time: 45.6 us; the launch traced here: 45.3 us
  Pallas kernels  31.8 us (70%)
  local copies, waits for them, and re-layouts  9.51 us (21%)
  matrix products  3.29 us (7%)
  between operations  0.65 us (1%)
    pallas_call x1, Pallas kernels, gathered(): pl.pallas_call(functools.partial(routed_kernel, dims), out_shape=(jax.Sha...  31.8 us
    unnamed x13, local copies, waits for them, and re-layouts  9.51 us
    dot_general x1, matrix products, contract_rows(): lax.dot_general(left, right, (((0,), (0,)), ((), ())), preferred_element_...  3.29 us

profile of v1, /device:TPU:0, one launch (start us, length us, event | category | flops | bytes accessed | tf_op | source)
XLA Modules:
  0.0 45.3 jit_solution(12451262509392774985)
XLA Ops:
  0.6 0.8 %copy.11.rw_ref = bf16[8,4]{1,0:T(8,128)(2,1)S(1)} copy(bf16[8,4]{0,1:T(4,128)(2,1)} %param.8) | data formatting | bytes 128 | tf_op args[2]
  1.4 0.8 %copy.10.ids_ref = s32[8,4]{1,0:T(8,128)S(1)} copy(s32[8,4]{0,1:T(4,128)} %param.7) | data formatting | bytes 256 | tf_op args[1]
  2.2 0.0 copy-start
  2.2 3.4 %copy-done = bf16[4096,1024]{1,0:T(8,128)(2,1)S(1)} copy-done((bf16[4096,1024]{1,0:T(8,128)(2,1)S(1)}, bf16[4096,1024]{1,0:T(8,128)(2,1)}, u32[]{:S(2)}) %copy-start) | copy-done | bytes 8388632
  5.5 0.0 copy-start.1
  5.5 0.9 %copy-done.1 = bf16[64,1024]{1,0:T(8,128)(2,1)S(1)} copy-done((bf16[64,1024]{1,0:T(8,128)(2,1)S(1)}, bf16[64,1024]{1,0:T(8,128)(2,1)}, u32[]{:S(2)}) %copy-start.1) | copy-done | bytes 131096
  6.4 0.0 copy-start.2
  6.4 0.9 %copy-done.2 = bf16[64,1024]{1,0:T(8,128)(2,1)S(1)} copy-done((bf16[64,1024]{1,0:T(8,128)(2,1)S(1)}, bf16[64,1024]{1,0:T(8,128)(2,1)}, u32[]{:S(2)}) %copy-start.2) | copy-done | bytes 131096
  7.3 0.0 copy-start.3
  7.3 0.8 %copy-done.3 = bf16[8,4096]{1,0:T(8,128)(2,1)S(1)} copy-done((bf16[8,4096]{1,0:T(8,128)(2,1)S(1)}, bf16[8,4096]{1,0:T(8,128)(2,1)}, u32[]{:S(2)}) %copy-start.3) | copy-done | bytes 65560
  8.2 31.8 %routed.1 = (bf16[128,2048]{1,0:T(8,128)(2,1)S(1)}, bf16[128,1024]{1,0:T(8,128)(2,1)S(1)}, bf16[64,1024]{1,0:T(8,128)(2,1)S(1)}, bf16[64,1024]{1,0:T(8,128)(2,1)S(1)}, bf16[32,4]{1,0:T(8,128)(2,1)S(1)}) custom-call(s32[8,4]{1,0:T(8,128)S(1)} %copy.10.ids_ref, bf16[8,4]{1,0:T(8,128)(2,1)S(1)} %copy.11.rw_ref, bf16[8,4096]{1,0:T(8,128)(2,1)S(1)} %copy-done.3, ...), custom_call_target="tpu_custom_call" | custom-call | tf_op jit(solution)/shard_map/routed/pallas_call | solution.py:309
  40.0 0.7 %copy.12 = bf16[32,4]{0,1:T(4,128)(2,1)} copy(bf16[32,4]{1,0:T(8,128)(2,1)S(1)} %get-tuple-element.17) | data formatting | bytes 512
  40.7 3.3 %convolution_convert_fusion = bf16[2048,1024]{1,0:T(8,128)(2,1)} fusion(bf16[128,2048]{1,0:T(8,128)(2,1)S(1)} %get-tuple-element.11, bf16[128,1024]{1,0:T(8,128)(2,1)S(1)} %get-tuple-element.12), kind=kOutput, calls=%fused_computation | convolution fusion | flops 538968064 | bytes 4980736 | tf_op jit(solution)/shard_map/dot_general | solution.py:19
  44.0 0.7 %copy.15 = bf16[64,1024]{1,0:T(8,128)(2,1)} copy(bf16[64,1024]{1,0:T(8,128)(2,1)S(1)} %get-tuple-element.22) | data formatting | bytes 262144
  44.6 0.7 %copy.16 = bf16[64,1024]{1,0:T(8,128)(2,1)} copy(bf16[64,1024]{1,0:T(8,128)(2,1)S(1)} %get-tuple-element.23) | data formatting | bytes 262144
Async XLA Ops:
  2.2 3.4 %copy-start = (bf16[4096,1024]{1,0:T(8,128)(2,1)S(1)}, bf16[4096,1024]{1,0:T(8,128)(2,1)}, u32[]{:S(2)}) copy-start(bf16[4096,1024]{1,0:T(8,128)(2,1)} %w_ref.1) | copy-start | bytes 25165828
  5.5 0.9 %copy-start.1 = (bf16[64,1024]{1,0:T(8,128)(2,1)S(1)}, bf16[64,1024]{1,0:T(8,128)(2,1)}, u32[]{:S(2)}) copy-start(bf16[64,1024]{1,0:T(8,128)(2,1)} %gate_ref.1) | copy-start | bytes 393220
  6.4 0.9 %copy-start.2 = (bf16[64,1024]{1,0:T(8,128)(2,1)S(1)}, bf16[64,1024]{1,0:T(8,128)(2,1)}, u32[]{:S(2)}) copy-start(bf16[64,1024]{1,0:T(8,128)(2,1)} %up_ref.1) | copy-start | bytes 393220
  7.3 0.8 %copy-start.3 = (bf16[8,4096]{1,0:T(8,128)(2,1)S(1)}, bf16[8,4096]{1,0:T(8,128)(2,1)}, u32[]{:S(2)}) copy-start(bf16[8,4096]{1,0:T(8,128)(2,1)} %grad_ref.1) | copy-start | bytes 196612

commit v2 on v1

--- a/solution.py
+++ b/solution.py
@@ -9,6 +9,7 @@
 H = 1024
 PER_GROUP = 2
 CHUNKS = 4
+DOWN_STEPS = 8
 MESH = pl.DeviceIdType.MESH
 F32 = jnp.float32
 BF16 = jnp.bfloat16
@@ -19,21 +20,31 @@
     return lax.dot_general(left, right, (((0,), (0,)), ((), ())), preferred_element_type=F32)
 
 
-def one_hot(member, column, width):
-    lanes = lax.broadcasted_iota(jnp.int32, (member.shape[0], width), 1).astype(F32)
-    return jnp.where((member > 0) & (column == lanes), 1.0, 0.0).astype(BF16)
-
-
-def lower_triangle(rows, block):
-    row = lax.broadcasted_iota(jnp.int32, (rows, rows), 0)
-    col = lax.broadcasted_iota(jnp.int32, (rows, rows), 1)
-    return jnp.where((col < row) & (row // block == col // block), 1.0, 0.0).astype(BF16)
+def one_hot(member, row, height):
+    places = lax.broadcasted_iota(jnp.int32, (height, member.shape[1]), 0).astype(F32)
+    return jnp.where((member > 0) & (row == places), 1.0, 0.0)
+
+
+def earlier_counts(rows, block):
+    count = rows.shape[1]
+    above = lax.broadcasted_iota(jnp.int32, (count, count), 0)
+    col = lax.broadcasted_iota(jnp.int32, (count, count), 1)
+    strict = jnp.where((above < col) & (above // block == col // block), 1.0, 0.0).astype(BF16)
+    return jnp.dot(rows.astype(BF16), strict, preferred_element_type=F32)
+
+
+def stacked(rows):
+    lines = lax.broadcasted_iota(jnp.int32, (8, rows[0].shape[1]), 0)
+    out = jnp.zeros(lines.shape, F32)
+    for place, row in enumerate(rows):
+        out = jnp.where(lines == place, row, out)
+    return out
 
 
 def routed_kernel(
     dims, ids_ref, rw_ref, grad_ref, gate_ref, up_ref, w_ref,
-    cot_out, wtd_out, ggate_out, gup_out, route_out,
-    ids_buf, rw_buf, coh, gath, peer_cot, w_buf, gate_buf, up_buf, acc, share_buf, back_buf,
+    cot_out, wtd_out, back_out, weight_out, route_out,
+    ids_buf, rw_buf, coh, gath, peer_cot, w_buf, gate_buf, up_buf, acc, hidden_buf, share_buf, back_buf,
     load_sem, w_sem, own_sem,
     ids_send, ids_recv, rw_send, rw_recv, coh_send, coh_recv,
     zids_send, zids_recv, zrw_send, zrw_recv,
@@ -90,11 +101,11 @@
     ]
     pl.semaphore_wait(barrier, nodes + locals_ - 1)
 
-    ids_copies, rw_copies, coh_copies = [], [], {}
+    meta_copies, coh_copies = [], {}
     for k in range(1, nodes):
-        ids_copies.append(remote(ids_ref, ids_buf.at[me_l, me_n], ids_send.at[k], ids_recv.at[k], node_at(k)))
-        rw_copies.append(remote(rw_ref, rw_buf.at[me_l, me_n], rw_send.at[k], rw_recv.at[k], node_at(k)))
-    for copy in ids_copies + rw_copies:
+        meta_copies.append(remote(ids_ref, ids_buf.at[me_l, me_n], ids_send.at[k], ids_recv.at[k], node_at(k)))
+        meta_copies.append(remote(rw_ref, rw_buf.at[me_l, me_n], rw_send.at[k], rw_recv.at[k], node_at(k)))
+    for copy in meta_copies:
         copy.start()
     for c in range(CHUNKS):
         for k in range(1, nodes):
@@ -108,25 +119,26 @@
         copy.start()
     for copy in own_copies:
         copy.wait()
-    for copy in ids_copies + rw_copies:
+    for copy in meta_copies:
         copy.wait_recv()
-    zids_copies, zrw_copies = [], []
+    zmeta_copies = []
     for k in range(1, locals_):
-        zids_copies.append(remote(ids_buf.at[me_l], ids_buf.at[me_l], zids_send.at[k], zids_recv.at[k], local_at(k)))
-        zrw_copies.append(remote(rw_buf.at[me_l], rw_buf.at[me_l], zrw_send.at[k], zrw_recv.at[k], local_at(k)))
-    for copy in zids_copies + zrw_copies:
+        zmeta_copies.append(remote(ids_buf.at[me_l], ids_buf.at[me_l], zids_send.at[k], zids_recv.at[k], local_at(k)))
+        zmeta_copies.append(remote(rw_buf.at[me_l], rw_buf.at[me_l], zrw_send.at[k], zrw_recv.at[k], local_at(k)))
+    for copy in zmeta_copies:
         copy.start()
 
-    own_ids = ids_buf[me_l].reshape(cohort, top)
-    lanes = lax.broadcasted_iota(jnp.int32, (cohort, 128), 1)
+    own = ids_buf[me_l].astype(F32)
+    own_ids = jnp.concatenate([own[n] for n in range(nodes)], axis=1)
     first = me_n * exp_group
-    hits = jnp.zeros((cohort, 128), F32)
-    for k in range(top):
-        hits = hits + jnp.where((own_ids[:, k:k + 1] - first == lanes) & (lanes < exp_group), 1.0, 0.0)
-    in_group = jnp.where(jnp.sum(hits, axis=1, keepdims=True) > 0, 1.0, 0.0)
-    hits = jnp.where(lanes == exp_group, in_group, hits)
-    before = jnp.dot(lower_triangle(cohort, cohort), hits.astype(BF16), preferred_element_type=F32)
-    pick = one_hot(in_group, before[:, exp_group:exp_group + 1], group_tok)
+    low = first.astype(F32)
+    hits = [
+        jnp.sum(jnp.where(own_ids == low + j, 1.0, 0.0), axis=0, keepdims=True)
+        for j in range(exp_group)
+    ]
+    in_group = jnp.where(sum(hits) > 0, 1.0, 0.0)
+    before = earlier_counts(stacked(hits + [in_group]), cohort)
+    pick = one_hot(in_group, before[exp_group:exp_group + 1], group_tok).astype(BF16)
 
     def shifted(buf, copies_send, copies_recv, source, d, c, step):
         return remote(
@@ -143,30 +155,33 @@
     state = {}
 
     def prepare():
-        for copy in zids_copies + zrw_copies:
+        for copy in zmeta_copies:
             copy.wait_recv()
         total = locals_ * cohort
-        all_ids = ids_buf[...].reshape(total, top)
-        all_rw = rw_buf[...].astype(F32).reshape(total, top)
-        expert = first + me_l // owners
-        match = jnp.where(all_ids == expert, 1.0, 0.0)
-        member = jnp.sum(match, axis=1, keepdims=True)
-        row_weight = jnp.sum(match * all_rw, axis=1, keepdims=True)
-        near = jnp.where((all_ids >= first) & (all_ids < first + exp_group), 1.0, 0.0)
-        grouped = jnp.where(jnp.sum(near, axis=1, keepdims=True) > 0, 1.0, 0.0)
-        lane = lax.broadcasted_iota(jnp.int32, (total, 128), 1)
-        both = jnp.where(lane == 0, member, jnp.where(lane == 1, grouped, 0.0)).astype(BF16)
-        earlier = jnp.dot(lower_triangle(total, cohort), both, preferred_element_type=F32)
-        which = (lax.broadcasted_iota(jnp.int32, (total, 1), 0) // cohort).astype(F32)
-        slot_hot = one_hot(member, earlier[:, 0:1] + which * capacity, slots)
-        pack_hot = one_hot(grouped, earlier[:, 1:2] + which * group_tok, locals_ * group_tok)
-        state["select"] = contract_rows(slot_hot, pack_hot).astype(BF16)
-        weight = contract_rows(slot_hot, jnp.broadcast_to(row_weight, (total, 128)).astype(BF16))[:, 0:1]
-        state["weight"] = weight
+        ids_all, rw_all = ids_buf[...].astype(F32), rw_buf[...].astype(F32)
+        places = [(l, n) for l in range(locals_) for n in range(nodes)]
+        all_ids = jnp.concatenate([ids_all[place] for place in places], axis=1)
+        all_rw = jnp.concatenate([rw_all[place] for place in places], axis=1)
+        match = jnp.where(all_ids == (first + me_l // owners).astype(F32), 1.0, 0.0)
+        member = jnp.sum(match, axis=0, keepdims=True)
+        row_weight = jnp.sum(match * all_rw, axis=0, keepdims=True)
+        near = jnp.where((all_ids >= low) & (all_ids < low + exp_group), 1.0, 0.0)
+        grouped = jnp.where(jnp.sum(near, axis=0, keepdims=True) > 0, 1.0, 0.0)
+        earlier = earlier_counts(stacked([member, grouped]), cohort)
+        which = (lax.broadcasted_iota(jnp.int32, (1, total), 1) // cohort).astype(F32)
+        slot_hot = one_hot(member, earlier[0:1] + which * capacity, slots)
+        pack_hot = one_hot(grouped, earlier[1:2] + which * group_tok, locals_ * group_tok)
+        state["select"] = lax.dot_general(
+            slot_hot.astype(BF16), pack_hot.astype(BF16),
+            (((1,), (1,)), ((), ())), preferred_element_type=F32,
+        ).astype(BF16)
+        weight = jnp.sum(slot_hot * row_weight, axis=1, keepdims=True)
+        weight_out[...] = jnp.broadcast_to(weight, (slots, 128))
         gate_copy.wait()
         up_copy.wait()
         gate = gate_buf[...].astype(F32)
         hidden = gate * jax.nn.sigmoid(gate) * up_buf[...].astype(F32)
+        hidden_buf[...] = hidden
         wtd_out[0:slots, :] = (weight * hidden).astype(BF16)
 
     wtd_copy = remote(wtd_out.at[0:slots, :], wtd_out.at[slots:2 * slots, :], wtd_send, wtd_recv, peer)
@@ -207,7 +222,8 @@
             for k in range(1, nodes):
                 coh_copies[step, k].wait_recv()
             rows = coh[:, :, cols(step)].astype(F32).reshape(cohort, cw).astype(BF16)
-            gath[me_l, :, cols(step)] = contract_rows(pick, rows).astype(BF16)
+            packed = jnp.dot(pick, rows, preferred_element_type=F32)
+            gath[me_l, :, cols(step)] = packed.astype(BF16)
 
             @pl.when(me_l + 1 < locals_)
             def _():
@@ -245,17 +261,9 @@
             if step == locals_ - 1:
                 wtd_copy.start()
 
-    weight = state["weight"]
-    gate = gate_buf[...].astype(F32)
-    up = up_buf[...].astype(F32)
     back = acc[...]
-    sig = jax.nn.sigmoid(gate)
-    act = gate * sig
-    shares = jnp.sum(act * up * back, axis=1, keepdims=True)
+    shares = jnp.sum(hidden_buf[...] * back, axis=1, keepdims=True)
     share_buf[...] = jnp.broadcast_to(shares, (slots, 128)).astype(BF16).reshape(locals_, capacity, 128)
-    scaled = weight * back
-    ggate_out[...] = (scaled * up * sig * (1.0 + gate * (1.0 - sig))).astype(BF16)
-    gup_out[...] = (scaled * act).astype(BF16)
     back_buf[me_l] = share_buf[me_l]
     share_copies = [
         remote(share_buf.at[lax.rem(me_l + k, locals_)], back_buf.at[me_l], share_send.at[k], share_recv.at[k], local_at(k))
@@ -263,8 +271,9 @@
     ]
     for copy in share_copies:
         copy.start()
-
-    for copy in ids_copies + rw_copies + zids_copies + zrw_copies + list(coh_copies.values()):
+    back_out[...] = back
+
+    for copy in meta_copies + zmeta_copies + list(coh_copies.values()):
         copy.wait_send()
     for c in range(CHUNKS):
         @pl.when(me_l + 1 < locals_)
@@ -285,14 +294,27 @@
         cot_copy(c).wait()
     for copy in share_copies:
         copy.wait()
-    route = jnp.zeros((cohort, 128), F32)
+    route = []
     for j in range(exp_group):
-        chosen = one_hot(hits[:, j:j + 1], before[:, j:j + 1], capacity)
-        value = jnp.zeros((cohort, 128), F32)
+        chosen = one_hot(hits[j], before[j:j + 1], capacity)
+        value = jnp.zeros((capacity, 1), F32)
         for o in range(owners):
-            value = value + jnp.dot(chosen, back_buf[j * owners + o], preferred_element_type=F32)
-        route = jnp.where(lanes == j, value, route)
-    route_out[...] = route[:, 0:exp_group].astype(BF16)
+            value = value + back_buf[j * owners + o, :, 0:1].astype(F32)
+        route.append(jnp.sum(chosen * value, axis=0, keepdims=True))
+    route_out[...] = stacked(route)
+
+
+def gradient_kernel(exp_group, cot, wtd, back_in, weight, route, gate_in, up_in, ggate, gup, down, groute):
+    down[...] = contract_rows(cot[...], wtd[...]).astype(BF16)
+
+    @pl.when(pl.program_id(0) == 0)
+    def _():
+        gate = gate_in[...].astype(F32)
+        sig = jax.nn.sigmoid(gate)
+        scaled = weight[:, 0:1] * back_in[...]
+        ggate[...] = (scaled * up_in[...].astype(F32) * sig * (1.0 + gate * (1.0 - sig))).astype(BF16)
+        gup[...] = (scaled * gate * sig).astype(BF16)
+        groute[...] = route[0:exp_group, :].astype(BF16)
 
 
 def gathered(nodes, locals_, group_tok, grad_out, expert_ids, route_weights, gate_pre, up_pre, w_down_t):
@@ -306,26 +328,28 @@
     half = width // 2
     dims = (nodes, locals_, tok, top, width, hs, group_tok, owners)
     dma = pltpu.SemaphoreType.DMA
-    cot, weighted, grad_gate, grad_up, grad_route = pl.pallas_call(
+    hbm = pl.BlockSpec(memory_space=pltpu.HBM)
+    cot, weighted, back, weight, route = pl.pallas_call(
         functools.partial(routed_kernel, dims),
         out_shape=(
             jax.ShapeDtypeStruct((2 * slots, half), BF16),
             jax.ShapeDtypeStruct((2 * slots, hs), BF16),
-            jax.ShapeDtypeStruct((slots, hs), BF16),
-            jax.ShapeDtypeStruct((slots, hs), BF16),
-            jax.ShapeDtypeStruct((cohort, exp_group), BF16),
+            jax.ShapeDtypeStruct((slots, hs), F32),
+            jax.ShapeDtypeStruct((slots, 128), F32),
+            jax.ShapeDtypeStruct((8, cohort), F32),
         ),
-        in_specs=[pl.BlockSpec(memory_space=pl.ANY)] * 6,
+        in_specs=[hbm] * 6,
         out_specs=tuple([pl.BlockSpec(memory_space=pltpu.VMEM)] * 5),
         scratch_shapes=[
-            pltpu.VMEM((locals_, nodes, tok, top), jnp.int32),
-            pltpu.VMEM((locals_, nodes, tok, top), BF16),
+            pltpu.VMEM((locals_, nodes, top, tok), jnp.int32),
+            pltpu.VMEM((locals_, nodes, top, tok), BF16),
             pltpu.VMEM((nodes, tok, width), BF16),
             pltpu.VMEM((locals_, group_tok, width), BF16),
             pltpu.VMEM((slots, half), BF16),
             pltpu.VMEM((width, hs), BF16),
             pltpu.VMEM((slots, hs), BF16),
             pltpu.VMEM((slots, hs), BF16),
+            pltpu.VMEM((slots, hs), F32),
             pltpu.VMEM((slots, hs), F32),
             pltpu.VMEM((locals_, capacity, 128), BF16),
             pltpu.VMEM((locals_, capacity, 128), BF16),
@@ -340,9 +364,35 @@
         ],
         compiler_params=pltpu.CompilerParams(collective_id=0, has_side_effects=True, **KERNEL_PARAMS),
         name="routed",
-    )(expert_ids, route_weights, grad_out, gate_pre, up_pre, w_down_t)
-    grad_down = contract_rows(cot, weighted).astype(BF16)
-    return grad_gate, grad_up, grad_down, grad_route
+    )(*[
+        pltpu.with_memory_space_constraint(x, pltpu.HBM)
+        for x in (expert_ids.T, route_weights.T, grad_out, gate_pre, up_pre, w_down_t)
+    ])
+    tile = half // DOWN_STEPS
+    vmem = pl.BlockSpec(memory_space=pltpu.VMEM)
+    grad_gate, grad_up, grad_down, grad_route = pl.pallas_call(
+        functools.partial(gradient_kernel, exp_group),
+        grid=(DOWN_STEPS,),
+        out_shape=(
+            jax.ShapeDtypeStruct((slots, hs), BF16),
+            jax.ShapeDtypeStruct((slots, hs), BF16),
+            jax.ShapeDtypeStruct((half, hs), BF16),
+            jax.ShapeDtypeStruct((exp_group, cohort), BF16),
+        ),
+        in_specs=[
+            pl.BlockSpec((2 * slots, tile), lambda i: (0, i)),
+            vmem, vmem, vmem, vmem, vmem, vmem,
+        ],
+        out_specs=(
+            pl.BlockSpec((slots, hs), lambda i: (0, 0)),
+            pl.BlockSpec((slots, hs), lambda i: (0, 0)),
+            pl.BlockSpec((tile, hs), lambda i: (i, 0)),
+            pl.BlockSpec((exp_group, cohort), lambda i: (0, 0)),
+        ),
+        compiler_params=pltpu.CompilerParams(vmem_limit_bytes=24 * 1024 * 1024),
+        name="gradients",
+    )(cot, weighted, back, weight, route, gate_pre, up_pre)
+    return grad_gate, grad_up, grad_down, grad_route.T
 
 
 def swapped(block, axis, distance):

time: 45.6 us -> 37.2 us (0.82)
  local copies, waits for them, and re-layouts: 9.51 us -> 0.01 us
  Pallas kernels: 31.8 us -> 36.4 us
  matrix products: 3.29 us -> 0 us
    unnamed x13 -> x4, local copies, waits for them, and re-layouts: 9.51 us -> 0.01 us
    pallas_call x0 -> x1, Pallas kernels: none -> 5.12 us  [gathered(): pl.pallas_call(functools.partial(gradient_kernel, exp_group), grid=(DOWN_...]
    dot_general x1 -> x0, matrix products: 3.29 us -> none  [contract_rows(): lax.dot_general(left, right, (((0,), (0,)), ((), ())), preferred_element_...]
    pallas_call x1, Pallas kernels: 31.8 us -> 31.3 us  [gathered(): pl.pallas_call(functools.partial(routed_kernel, dims), out_shape=(jax.Sha...]
where the time goes in v2:
time: 37.2 us; the launch traced here: 37.1 us
  Pallas kernels  36.4 us (98%)
  between operations  0.67 us (2%)
    pallas_call x1, Pallas kernels, gathered(): pl.pallas_call(functools.partial(routed_kernel, dims), out_shape=(jax.Sha...  31.3 us
    pallas_call x1, Pallas kernels, gathered(): pl.pallas_call(functools.partial(gradient_kernel, exp_group), grid=(DOWN_...  5.12 us

profile of v2, /device:TPU:0, one launch (start us, length us, event | category | flops | bytes accessed | tf_op | source)
XLA Modules:
  0.0 37.1 jit_solution(10508448014326240423)
XLA Ops:
  0.6 0.0 copy-start.1
  0.6 0.0 copy-start
  0.7 31.3 %routed.1 = (bf16[128,2048]{1,0:T(8,128)(2,1)S(1)}, bf16[128,1024]{1,0:T(8,128)(2,1)S(1)}, f32[64,1024]{1,0:T(8,128)S(1)}, f32[64,128]{1,0:T(8,128)S(1)}, f32[8,32]{1,0:T(8,128)S(1)}) custom-call(s32[4,8]{1,0:T(4,128)} %bitcast.3, bf16[4,8]{1,0:T(4,128)(2,1)} %bitcast.4, bf16[8,4096]{1,0:T(8,128)(2,1)} %grad_ref.1, bf16[64,1024]{1,0:T(8,128)(2,1)} %gate_in.1, ...), custom_call_target="tpu_custom_call" | custom-call | tf_op jit(solution)/shard_map/routed/pallas_call | solution.py:332
  31.9 0.0 copy-done.1
  31.9 0.0 copy-done
  32.0 5.1 %gradients.1 = (bf16[64,1024]{1,0:T(8,128)(2,1)}, bf16[64,1024]{1,0:T(8,128)(2,1)}, bf16[2048,1024]{1,0:T(8,128)(2,1)}, bf16[4,32]{1,0:T(4,128)(2,1)}) custom-call(bf16[128,2048]{1,0:T(8,128)(2,1)S(1)} %get-tuple-element.13.cot, bf16[128,1024]{1,0:T(8,128)(2,1)S(1)} %get-tuple-element.14.wtd, f32[64,1024]{1,0:T(8,128)S(1)} %get-tuple-element.15.back_in, ...), custom_call_target="tpu_custom_call" | custom-call | tf_op jit(solution)/shard_map/gradients/pallas_call | solution.py:373
Async XLA Ops:
  0.6 31.3 %copy-start.1 = (bf16[64,1024]{1,0:T(8,128)(2,1)S(1)}, bf16[64,1024]{1,0:T(8,128)(2,1)}, u32[]{:S(2)}) copy-start(bf16[64,1024]{1,0:T(8,128)(2,1)} %up_in.1) | copy-start | bytes 393220
  0.6 31.3 %copy-start = (bf16[64,1024]{1,0:T(8,128)(2,1)S(1)}, bf16[64,1024]{1,0:T(8,128)(2,1)}, u32[]{:S(2)}) copy-start(bf16[64,1024]{1,0:T(8,128)(2,1)} %gate_in.1) | copy-start | bytes 393220

commit v3 on v2

--- a/solution.py
+++ b/solution.py
@@ -9,7 +9,7 @@
 H = 1024
 PER_GROUP = 2
 CHUNKS = 4
-DOWN_STEPS = 8
+TILES = 4
 MESH = pl.DeviceIdType.MESH
 F32 = jnp.float32
 BF16 = jnp.bfloat16
@@ -43,8 +43,8 @@
 
 def routed_kernel(
     dims, ids_ref, rw_ref, grad_ref, gate_ref, up_ref, w_ref,
-    cot_out, wtd_out, back_out, weight_out, route_out,
-    ids_buf, rw_buf, coh, gath, peer_cot, w_buf, gate_buf, up_buf, acc, hidden_buf, share_buf, back_buf,
+    ggate_out, gup_out, down_out, route_out,
+    cot_out, wtd_out, ids_buf, rw_buf, coh, gath, peer_cot, w_buf, gate_buf, up_buf, acc, hidden_buf, share_buf, back_buf,
     load_sem, w_sem, own_sem,
     ids_send, ids_recv, rw_send, rw_recv, coh_send, coh_recv,
     zids_send, zids_recv, zrw_send, zrw_recv,
@@ -82,7 +82,7 @@
     pl.semaphore_signal(barrier, inc=1, device_id=peer, device_id_type=MESH)
 
     def cols(c):
-        return pl.ds(c * cw, cw)
+        return pl.ds((c % 2) * half + (c // 2) * cw, cw)
 
     own_copies = [
         pltpu.make_async_copy(ids_ref, ids_buf.at[me_l, me_n], own_sem.at[0]),
@@ -176,7 +176,7 @@
             (((1,), (1,)), ((), ())), preferred_element_type=F32,
         ).astype(BF16)
         weight = jnp.sum(slot_hot * row_weight, axis=1, keepdims=True)
-        weight_out[...] = jnp.broadcast_to(weight, (slots, 128))
+        state["weight"] = weight
         gate_copy.wait()
         up_copy.wait()
         gate = gate_buf[...].astype(F32)
@@ -187,22 +187,22 @@
     wtd_copy = remote(wtd_out.at[0:slots, :], wtd_out.at[slots:2 * slots, :], wtd_send, wtd_recv, peer)
 
     def cot_copy(c):
-        part = pl.ds((c % half_chunks) * cw, cw)
+        part = pl.ds(c // 2 * cw, cw)
         return remote(
             peer_cot.at[:, part], cot_out.at[slots:2 * slots, part],
-            cot_send.at[c % half_chunks], cot_recv.at[c % half_chunks], peer,
+            cot_send.at[c // 2], cot_recv.at[c // 2], peer,
         )
 
     def finish(c):
         rows = gath[:, :, cols(c)].reshape(locals_ * group_tok, cw)
         cot = jnp.dot(state["select"], rows, preferred_element_type=F32).astype(BF16)
-        part = pl.ds((c % half_chunks) * cw, cw)
-
-        @pl.when(me_r == c // half_chunks)
+        part = pl.ds(c // 2 * cw, cw)
+
+        @pl.when(me_r == c % 2)
         def _():
             cot_out[0:slots, part] = cot
 
-        @pl.when(me_r != c // half_chunks)
+        @pl.when(me_r != c % 2)
         def _():
             peer_cot[:, part] = cot
 
@@ -213,9 +213,18 @@
         else:
             acc[...] += term
 
-        @pl.when(me_r != c // half_chunks)
+        @pl.when(me_r != c % 2)
         def _():
             cot_copy(c).start()
+
+    def outer(p):
+        if p == 0:
+            wtd_copy.wait_recv()
+        cot_copy(2 * p).wait_recv()
+        tile = cw // TILES
+        for t in range(TILES):
+            place = pl.ds(p * cw + t * tile, tile)
+            down_out[place, :] = contract_rows(cot_out[:, place], wtd_out[...]).astype(BF16)
 
     for step in range(CHUNKS + locals_ - 1):
         if step < CHUNKS:
@@ -257,9 +266,12 @@
         if step == locals_ - 2:
             prepare()
         if step >= locals_ - 1:
-            finish(step - locals_ + 1)
-            if step == locals_ - 1:
+            done = step - locals_ + 1
+            finish(done)
+            if done == 0:
                 wtd_copy.start()
+            if done % 2 == 0 and done > 0:
+                outer(done // 2 - 1)
 
     back = acc[...]
     shares = jnp.sum(hidden_buf[...] * back, axis=1, keepdims=True)
@@ -271,7 +283,12 @@
     ]
     for copy in share_copies:
         copy.start()
-    back_out[...] = back
+    gate = gate_buf[...].astype(F32)
+    sig = jax.nn.sigmoid(gate)
+    scaled = state["weight"] * back
+    ggate_out[...] = (scaled * up_buf[...].astype(F32) * sig * (1.0 + gate * (1.0 - sig))).astype(BF16)
+    gup_out[...] = (scaled * gate * sig).astype(BF16)
+    outer(half_chunks - 1)
 
     for copy in meta_copies + zmeta_copies + list(coh_copies.values()):
         copy.wait_send()
@@ -289,9 +306,9 @@
                 @pl.when(me_l + d < locals_)
                 def _():
                     left(me_l + d, d + 1, c).wait_send()
-    wtd_copy.wait()
-    for c in range(half_chunks):
-        cot_copy(c).wait()
+    wtd_copy.wait_send()
+    for p in range(half_chunks):
+        cot_copy(2 * p).wait_send()
     for copy in share_copies:
         copy.wait()
     route = []
@@ -301,20 +318,21 @@
         for o in range(owners):
             value = value + back_buf[j * owners + o, :, 0:1].astype(F32)
         route.append(jnp.sum(chosen * value, axis=0, keepdims=True))
-    route_out[...] = stacked(route)
-
-
-def gradient_kernel(exp_group, cot, wtd, back_in, weight, route, gate_in, up_in, ggate, gup, down, groute):
-    down[...] = contract_rows(cot[...], wtd[...]).astype(BF16)
-
-    @pl.when(pl.program_id(0) == 0)
-    def _():
-        gate = gate_in[...].astype(F32)
-        sig = jax.nn.sigmoid(gate)
-        scaled = weight[:, 0:1] * back_in[...]
-        ggate[...] = (scaled * up_in[...].astype(F32) * sig * (1.0 + gate * (1.0 - sig))).astype(BF16)
-        gup[...] = (scaled * gate * sig).astype(BF16)
-        groute[...] = route[0:exp_group, :].astype(BF16)
+    route_out[...] = stacked(route)[0:exp_group].astype(BF16)
+
+
+def write_kernel(gate_in, up_in, down_in, route_in, gate_to, up_to, down_to, route_to, sems, down_sems):
+    rows = down_in.shape[0] // (2 * TILES)
+    copies = [
+        pltpu.make_async_copy(down_in.at[pl.ds(t * rows, rows)], down_to.at[pl.ds(t * rows, rows)], down_sems.at[t])
+        for t in range(2 * TILES)
+    ]
+    pairs = ((gate_in, gate_to), (up_in, up_to), (route_in, route_to))
+    copies += [pltpu.make_async_copy(src, dst, sems.at[t]) for t, (src, dst) in enumerate(pairs)]
+    for copy in copies:
+        copy.start()
+    for copy in copies:
+        copy.wait()
 
 
 def gathered(nodes, locals_, group_tok, grad_out, expert_ids, route_weights, gate_pre, up_pre, w_down_t):
@@ -329,18 +347,20 @@
     dims = (nodes, locals_, tok, top, width, hs, group_tok, owners)
     dma = pltpu.SemaphoreType.DMA
     hbm = pl.BlockSpec(memory_space=pltpu.HBM)
-    cot, weighted, back, weight, route = pl.pallas_call(
+    shapes = (
+        jax.ShapeDtypeStruct((slots, hs), BF16),
+        jax.ShapeDtypeStruct((slots, hs), BF16),
+        jax.ShapeDtypeStruct((half, hs), BF16),
+        jax.ShapeDtypeStruct((exp_group, cohort), BF16),
+    )
+    results = pl.pallas_call(
         functools.partial(routed_kernel, dims),
-        out_shape=(
-            jax.ShapeDtypeStruct((2 * slots, half), BF16),
-            jax.ShapeDtypeStruct((2 * slots, hs), BF16),
-            jax.ShapeDtypeStruct((slots, hs), F32),
-            jax.ShapeDtypeStruct((slots, 128), F32),
-            jax.ShapeDtypeStruct((8, cohort), F32),
-        ),
+        out_shape=shapes,
         in_specs=[hbm] * 6,
-        out_specs=tuple([pl.BlockSpec(memory_space=pltpu.VMEM)] * 5),
+        out_specs=tuple([pl.BlockSpec(memory_space=pltpu.VMEM)] * 4),
         scratch_shapes=[
+            pltpu.VMEM((2 * slots, half), BF16),
+            pltpu.VMEM((2 * slots, hs), BF16),
             pltpu.VMEM((locals_, nodes, top, tok), jnp.int32),
             pltpu.VMEM((locals_, nodes, top, tok), BF16),
             pltpu.VMEM((nodes, tok, width), BF16),
@@ -368,30 +388,15 @@
         pltpu.with_memory_space_constraint(x, pltpu.HBM)
         for x in (expert_ids.T, route_weights.T, grad_out, gate_pre, up_pre, w_down_t)
     ])
-    tile = half // DOWN_STEPS
-    vmem = pl.BlockSpec(memory_space=pltpu.VMEM)
     grad_gate, grad_up, grad_down, grad_route = pl.pallas_call(
-        functools.partial(gradient_kernel, exp_group),
-        grid=(DOWN_STEPS,),
-        out_shape=(
-            jax.ShapeDtypeStruct((slots, hs), BF16),
-            jax.ShapeDtypeStruct((slots, hs), BF16),
-            jax.ShapeDtypeStruct((half, hs), BF16),
-            jax.ShapeDtypeStruct((exp_group, cohort), BF16),
-        ),
-        in_specs=[
-            pl.BlockSpec((2 * slots, tile), lambda i: (0, i)),
-            vmem, vmem, vmem, vmem, vmem, vmem,
-        ],
-        out_specs=(
-            pl.BlockSpec((slots, hs), lambda i: (0, 0)),
-            pl.BlockSpec((slots, hs), lambda i: (0, 0)),
-            pl.BlockSpec((tile, hs), lambda i: (i, 0)),
-            pl.BlockSpec((exp_group, cohort), lambda i: (0, 0)),
-        ),
-        compiler_params=pltpu.CompilerParams(vmem_limit_bytes=24 * 1024 * 1024),
-        name="gradients",
-    )(cot, weighted, back, weight, route, gate_pre, up_pre)
+        write_kernel,
+        out_shape=shapes,
+        in_specs=[pl.BlockSpec(memory_space=pl.ANY)] * 4,
+        out_specs=tuple([pl.BlockSpec(memory_space=pl.ANY)] * 4),
+        scratch_shapes=[dma((3,)), dma((2 * TILES,))],
+        compiler_params=pltpu.CompilerParams(vmem_limit_bytes=1024 * 1024),
+        name="write",
+    )(*results)
     return grad_gate, grad_up, grad_down, grad_route.T
 
 

time: 37.2 us -> 34.3 us (0.922)
  Pallas kernels: 36.4 us -> 33.5 us
    pallas_call x2, Pallas kernels: 36.4 us -> 33.5 us  [the longest x1 31.3 us: gathered(): pl.pallas_call(functools.partial(routed_kernel, dims), out_shape=shapes,...]
where the time goes in v3:
time: 34.3 us; the launch traced here: 34.1 us
  Pallas kernels  33.5 us (98%)
  between operations  0.64 us (2%)
    pallas_call x1, Pallas kernels, gathered(): pl.pallas_call(functools.partial(routed_kernel, dims), out_shape=shapes,...  31.3 us
    pallas_call x1, Pallas kernels, gathered(): pl.pallas_call(write_kernel, out_shape=shapes, in_specs=[pl.BlockSpec(mem...  2.19 us

profile of v3, /device:TPU:0, one launch (start us, length us, event | category | flops | bytes accessed | tf_op | source)
XLA Modules:
  0.0 34.1 jit_solution(15558750643003674859)
XLA Ops:
  0.6 31.3 %routed.1 = (bf16[64,1024]{1,0:T(8,128)(2,1)S(1)}, bf16[64,1024]{1,0:T(8,128)(2,1)S(1)}, bf16[2048,1024]{1,0:T(8,128)(2,1)S(1)}, bf16[4,32]{1,0:T(4,128)(2,1)S(1)}) custom-call(s32[4,8]{1,0:T(4,128)} %bitcast.3, bf16[4,8]{1,0:T(4,128)(2,1)} %bitcast.4, bf16[8,4096]{1,0:T(8,128)(2,1)} %grad_ref.1, bf16[64,1024]{1,0:T(8,128)(2,1)} %gate_ref.1, ...), custom_call_target="tpu_custom_call" | custom-call | tf_op jit(solution)/shard_map/routed/pallas_call | solution.py:356
  31.9 2.2 %write.1 = (bf16[64,1024]{1,0:T(8,128)(2,1)}, bf16[64,1024]{1,0:T(8,128)(2,1)}, bf16[2048,1024]{1,0:T(8,128)(2,1)}, bf16[4,32]{1,0:T(4,128)(2,1)}) custom-call(bf16[64,1024]{1,0:T(8,128)(2,1)S(1)} %get-tuple-element.12.gate_in, bf16[64,1024]{1,0:T(8,128)(2,1)S(1)} %get-tuple-element.13.up_in, bf16[2048,1024]{1,0:T(8,128)(2,1)S(1)} %get-tuple-element.14.down_in, ...), custom_call_target="tpu_custom_call" | custom-call | tf_op jit(solution)/shard_map/write/pallas_call | solution.py:391

commit v4 on v3

--- a/solution.py
+++ b/solution.py
@@ -226,52 +226,51 @@
             place = pl.ds(p * cw + t * tile, tile)
             down_out[place, :] = contract_rows(cot_out[:, place], wtd_out[...]).astype(BF16)
 
-    for step in range(CHUNKS + locals_ - 1):
-        if step < CHUNKS:
-            for k in range(1, nodes):
-                coh_copies[step, k].wait_recv()
-            rows = coh[:, :, cols(step)].astype(F32).reshape(cohort, cw).astype(BF16)
-            packed = jnp.dot(pick, rows, preferred_element_type=F32)
-            gath[me_l, :, cols(step)] = packed.astype(BF16)
-
-            @pl.when(me_l + 1 < locals_)
-            def _():
-                right(me_l, 1, step).start()
-
-            @pl.when(me_l > 0)
-            def _():
-                left(me_l, 1, step).start()
-
-        for d in range(1, locals_):
-            c = step - d
-            if not 0 <= c < CHUNKS:
-                continue
-
-            @pl.when(me_l >= d)
-            def _():
-                right(me_l - d, d, c).wait_recv()
-                if d < locals_ - 1:
-                    @pl.when(me_l + 1 < locals_)
-                    def _():
-                        right(me_l - d, d + 1, c).start()
-
-            @pl.when(me_l + d < locals_)
-            def _():
-                left(me_l + d, d, c).wait_recv()
-                if d < locals_ - 1:
-                    @pl.when(me_l > 0)
-                    def _():
-                        left(me_l + d, d + 1, c).start()
-
-        if step == locals_ - 2:
+    def send_own(c):
+        for k in range(1, nodes):
+            coh_copies[c, k].wait_recv()
+        rows = coh[:, :, cols(c)].astype(F32).reshape(cohort, cw).astype(BF16)
+        packed = jnp.dot(pick, rows, preferred_element_type=F32)
+        gath[me_l, :, cols(c)] = packed.astype(BF16)
+
+        @pl.when(me_l + 1 < locals_)
+        def _():
+            right(me_l, 1, c).start()
+
+        @pl.when(me_l > 0)
+        def _():
+            left(me_l, 1, c).start()
+
+    def relay(d, c):
+        @pl.when(me_l >= d)
+        def _():
+            right(me_l - d, d, c).wait_recv()
+            if d < locals_ - 1:
+                @pl.when(me_l + 1 < locals_)
+                def _():
+                    right(me_l - d, d + 1, c).start()
+
+        @pl.when(me_l + d < locals_)
+        def _():
+            left(me_l + d, d, c).wait_recv()
+            if d < locals_ - 1:
+                @pl.when(me_l > 0)
+                def _():
+                    left(me_l + d, d + 1, c).start()
+
+    for c in range(CHUNKS):
+        send_own(c)
+    for d in range(1, locals_):
+        if d == locals_ - 1:
             prepare()
-        if step >= locals_ - 1:
-            done = step - locals_ + 1
-            finish(done)
-            if done == 0:
-                wtd_copy.start()
-            if done % 2 == 0 and done > 0:
-                outer(done // 2 - 1)
+        for c in range(CHUNKS):
+            relay(d, c)
+            if d == locals_ - 1:
+                finish(c)
+                if c == 0:
+                    wtd_copy.start()
+                if c % 2 == 0 and c > 0:
+                    outer(c // 2 - 1)
 
     back = acc[...]
     shares = jnp.sum(hidden_buf[...] * back, axis=1, keepdims=True)

time: 34.3 us -> 29.7 us (0.87)
  Pallas kernels: 33.5 us -> 28.9 us
    pallas_call x1, Pallas kernels: 31.3 us -> 26.7 us  [gathered(): pl.pallas_call(functools.partial(routed_kernel, dims), out_shape=shapes,...]
where the time goes in v4:
time: 29.7 us; the launch traced here: 29.5 us
  Pallas kernels  28.9 us (97%)
  between operations  0.64 us (2%)
    pallas_call x1, Pallas kernels, gathered(): pl.pallas_call(functools.partial(routed_kernel, dims), out_shape=shapes,...  26.7 us
    pallas_call x1, Pallas kernels, gathered(): pl.pallas_call(write_kernel, out_shape=shapes, in_specs=[pl.BlockSpec(mem...  2.19 us

profile of v4, /device:TPU:0, one launch (start us, length us, event | category | flops | bytes accessed | tf_op | source)
XLA Modules:
  0.0 29.5 jit_solution(7613630941950804428)
XLA Ops:
  0.6 26.7 %routed.1 = (bf16[64,1024]{1,0:T(8,128)(2,1)S(1)}, bf16[64,1024]{1,0:T(8,128)(2,1)S(1)}, bf16[2048,1024]{1,0:T(8,128)(2,1)S(1)}, bf16[4,32]{1,0:T(4,128)(2,1)S(1)}) custom-call(s32[4,8]{1,0:T(4,128)} %bitcast.3, bf16[4,8]{1,0:T(4,128)(2,1)} %bitcast.4, bf16[8,4096]{1,0:T(8,128)(2,1)} %grad_ref.1, bf16[64,1024]{1,0:T(8,128)(2,1)} %gate_ref.1, ...), custom_call_target="tpu_custom_call" | custom-call | tf_op jit(solution)/shard_map/routed/pallas_call | solution.py:355
  27.4 2.2 %write.1 = (bf16[64,1024]{1,0:T(8,128)(2,1)}, bf16[64,1024]{1,0:T(8,128)(2,1)}, bf16[2048,1024]{1,0:T(8,128)(2,1)}, bf16[4,32]{1,0:T(4,128)(2,1)}) custom-call(bf16[64,1024]{1,0:T(8,128)(2,1)S(1)} %get-tuple-element.12.gate_in, bf16[64,1024]{1,0:T(8,128)(2,1)S(1)} %get-tuple-element.13.up_in, bf16[2048,1024]{1,0:T(8,128)(2,1)S(1)} %get-tuple-element.14.down_in, ...), custom_call_target="tpu_custom_call" | custom-call | tf_op jit(solution)/shard_map/write/pallas_call | solution.py:390

commit v5 on v4

--- a/solution.py
+++ b/solution.py
@@ -269,8 +269,6 @@
                 finish(c)
                 if c == 0:
                     wtd_copy.start()
-                if c % 2 == 0 and c > 0:
-                    outer(c // 2 - 1)
 
     back = acc[...]
     shares = jnp.sum(hidden_buf[...] * back, axis=1, keepdims=True)
@@ -287,7 +285,8 @@
     scaled = state["weight"] * back
     ggate_out[...] = (scaled * up_buf[...].astype(F32) * sig * (1.0 + gate * (1.0 - sig))).astype(BF16)
     gup_out[...] = (scaled * gate * sig).astype(BF16)
-    outer(half_chunks - 1)
+    for p in range(half_chunks):
+        outer(p)
 
     for copy in meta_copies + zmeta_copies + list(coh_copies.values()):
         copy.wait_send()

time: 29.7 us -> 29 us (0.976)
  Pallas kernels: 28.9 us -> 28.2 us
    pallas_call x1, Pallas kernels: 26.7 us -> 26 us  [gathered(): pl.pallas_call(functools.partial(routed_kernel, dims), out_shape=shapes,...]
where the time goes in v5:
time: 29 us; the launch traced here: 28.8 us
  Pallas kernels  28.2 us (97%)
  between operations  0.64 us (2%)
    pallas_call x1, Pallas kernels, gathered(): pl.pallas_call(functools.partial(routed_kernel, dims), out_shape=shapes,...  26 us
    pallas_call x1, Pallas kernels, gathered(): pl.pallas_call(write_kernel, out_shape=shapes, in_specs=[pl.BlockSpec(mem...  2.19 us

profile of v5, /device:TPU:0, one launch (start us, length us, event | category | flops | bytes accessed | tf_op | source)
XLA Modules:
  0.0 28.8 jit_solution(1062799224026057507)
XLA Ops:
  0.6 26.0 %routed.1 = (bf16[64,1024]{1,0:T(8,128)(2,1)S(1)}, bf16[64,1024]{1,0:T(8,128)(2,1)S(1)}, bf16[2048,1024]{1,0:T(8,128)(2,1)S(1)}, bf16[4,32]{1,0:T(4,128)(2,1)S(1)}) custom-call(s32[4,8]{1,0:T(4,128)} %bitcast.3, bf16[4,8]{1,0:T(4,128)(2,1)} %bitcast.4, bf16[8,4096]{1,0:T(8,128)(2,1)} %grad_ref.1, bf16[64,1024]{1,0:T(8,128)(2,1)} %gate_ref.1, ...), custom_call_target="tpu_custom_call" | custom-call | tf_op jit(solution)/shard_map/routed/pallas_call | solution.py:354
  26.6 2.2 %write.1 = (bf16[64,1024]{1,0:T(8,128)(2,1)}, bf16[64,1024]{1,0:T(8,128)(2,1)}, bf16[2048,1024]{1,0:T(8,128)(2,1)}, bf16[4,32]{1,0:T(4,128)(2,1)}) custom-call(bf16[64,1024]{1,0:T(8,128)(2,1)S(1)} %get-tuple-element.12.gate_in, bf16[64,1024]{1,0:T(8,128)(2,1)S(1)} %get-tuple-element.13.up_in, bf16[2048,1024]{1,0:T(8,128)(2,1)S(1)} %get-tuple-element.14.down_in, ...), custom_call_target="tpu_custom_call" | custom-call | tf_op jit(solution)/shard_map/write/pallas_call | solution.py:389
